TPU v7x, 32 devices: a whole 2x2x4 slice. The times are simulated.
32 devices in a mesh: grp: 2 (over y), dev: 16 (over z, x, core).
Axes of the slice: x: 2, y: 2, z: 4, core: 2. Of those that a mesh axis runs over, the one named last changes fastest.
Arguments:
- spectra: bfloat16 [512, 2, 2048], P(('grp', 'dev')), may hold values from -6 to 6
- stack_in: bfloat16 [2, 256, 512, 128], P(None, None, ('grp', 'dev')), may hold values from -6 to 6
- plan: int32 [2], replicated, may hold values from 0 to 1
- seg_lengths: int32 [16], replicated, may hold values from 1 to 64, 512 in all
- taps: float32 [9], replicated, may hold values from -3 to 3
Outputs:
- stack: float32 [2, 256, 512, 128], P(None, None, ('grp', 'dev'))
- filtered: float32 [2, 256, 512, 128], P(None, None, ('grp', 'dev'))
All inputs are finite; a program needn't handle non-finite values.
Results may differ from a plain program's by a relative error of at most 0.0026.
Values may be sent and summed in bfloat16 or wider, within the bound.
No kernel may reach another device: no remote copies, remote signals or barrier semaphores. Data moves between devices by JAX's collectives and lax.ppermute only.
A program may use at most 64 MiB of HBM per device.

v0:
```python
import math
import jax
import jax.numpy as jnp
from jax import lax
from jax.sharding import PartitionSpec as P


def from_root(value, axis, source):
    kept = jnp.where(lax.axis_index(axis) == source, value, 0).astype(value.dtype)
    return lax.psum(kept, axis)


def extended_2(block, sides, width):
    for axis, dim in sides:
        count = lax.axis_size(axis)
        forward = [(i, i + 1) for i in range(count - 1)]
        backward = [(target, source) for source, target in forward]
        low = lax.ppermute(
            lax.slice_in_dim(block, block.shape[dim] - width, None, axis=dim), axis, forward
        )
        high = lax.ppermute(lax.slice_in_dim(block, 0, width, axis=dim), axis, backward)
        block = jnp.concatenate([low, block, high], axis=dim)
    return block


def whiten(spectra):
    real_part = spectra[:, 0, :].astype(jnp.float32)
    imag_part = spectra[:, 1, :].astype(jnp.float32)
    magnitude = jnp.sqrt(real_part * real_part + imag_part * imag_part)
    factor = 1.0 / jnp.maximum(magnitude, 0.25)
    return jnp.stack([real_part * factor, imag_part * factor], axis=1).astype(jnp.bfloat16)


def make_table(freqs, lags):
    bins = jnp.arange(freqs, dtype=jnp.int32)[:, None]
    shifts = jnp.arange(lags, dtype=jnp.int32)[None, :] - lags // 2
    modulus = bins * shifts % (2 * freqs)
    angle = modulus.astype(jnp.float32) * (math.pi / freqs)
    scale_value = 1.0 / math.sqrt(freqs)
    table = jnp.concatenate([jnp.cos(angle), -jnp.sin(angle)], axis=0) * scale_value
    return table.astype(jnp.bfloat16)


def cross_block(sources, receivers, table):
    src_re = sources[:, 0, :].astype(jnp.float32)[:, None, :]
    src_im = sources[:, 1, :].astype(jnp.float32)[:, None, :]
    rec_re = receivers[:, 0, :].astype(jnp.float32)[None, :, :]
    rec_im = receivers[:, 1, :].astype(jnp.float32)[None, :, :]
    cross_re = src_re * rec_re + src_im * rec_im
    cross_im = src_im * rec_re - src_re * rec_im
    cross = jnp.concatenate([cross_re, cross_im], axis=-1).astype(jnp.bfloat16)
    rows = sources.shape[0] * receivers.shape[0]
    flat = cross.reshape(rows, cross.shape[-1])
    result = jnp.dot(flat, table, preferred_element_type=jnp.float32)
    return result.reshape(sources.shape[0], receivers.shape[0], table.shape[1])


def segment_of(channel_ids, seg_lengths):
    bounds = jnp.cumsum(seg_lengths)[:-1]
    return jnp.sum((channel_ids[:, None] >= bounds[None, :]).astype(jnp.int32), axis=1)


def mixing_weights(seg_ids, taps, count):
    width = (taps.shape[0] - 1) // 2
    centre = seg_ids[width : width + count]
    columns = []
    for offset in range(taps.shape[0]):
        same = (seg_ids[offset : offset + count] == centre).astype(jnp.float32)
        columns.append(taps[offset] * same)
    return jnp.stack(columns, axis=1)


def apply_filter(extended, mixing, dim, count):
    total = jnp.zeros(extended.shape[:dim] + (count,) + extended.shape[dim + 1 :], jnp.float32)
    for offset in range(mixing.shape[1]):
        part = lax.slice_in_dim(extended, offset, offset + count, axis=dim)
        shape = [1] * extended.ndim
        shape[dim] = count
        total = total + mixing[:, offset].reshape(shape) * part
    return total


def shards(spectra, stack_in, plan, seg_lengths, taps):
    shard = spectra.shape[0]
    freqs = spectra.shape[2]
    steps = stack_in.shape[0]
    source_count = stack_in.shape[1]
    lags = stack_in.shape[3]
    width = (taps.shape[0] - 1) // 2
    group_channels = lax.axis_size("dev") * shard
    own = whiten(spectra)
    table = make_table(freqs, lags)
    block_rows = min(source_count, max(1, 512 // shard))
    start_channel = lax.axis_index(("grp", "dev")) * shard
    channel_ids = start_channel + jnp.arange(shard + 2 * width, dtype=jnp.int32) - width
    seg_ids = segment_of(channel_ids, seg_lengths)
    mixing = mixing_weights(seg_ids, taps, shard)
    stacks = []
    filtered_list = []
    for step in range(steps):
        first = plan[step] * source_count
        owner = first // group_channels
        offset = first % group_channels
        whole = lax.all_gather(own, "dev", axis=0, tiled=True)
        piece = lax.dynamic_slice_in_dim(whole, offset, source_count, 0)
        sources = from_root(piece, "grp", owner)
        grouped = sources.reshape(source_count // block_rows, block_rows, 2, freqs)
        corr = lax.map(lambda block: cross_block(block, own, table), grouped)
        corr = corr.reshape(source_count, shard, lags)
        updated = stack_in[step].astype(jnp.float32) + corr
        stacks.append(updated)
        extended = extended_2(updated, ((("grp", "dev"), 1),), width)
        filtered_list.append(apply_filter(extended, mixing, 1, shard))
    stack = jnp.stack(stacks, axis=0)
    filtered = jnp.stack(filtered_list, axis=0)
    return (stack, filtered)


def solution(mesh):
    placed = (P(("grp", "dev"), None, None), P(None, None, ("grp", "dev"), None), P(), P(), P())
    return jax.shard_map(
        shards,
        mesh=mesh,
        in_specs=placed,
        out_specs=(P(None, None, ("grp", "dev"), None), P(None, None, ("grp", "dev"), None)),
        check_vma=False,
    )
```

profile of v0, /device:TPU:1, one launch (start us, length us, event | category | flops | bytes accessed | tf_op | source)
XLA Modules:
  0.0 273.0 jit_solution(8880762887707342477)
XLA Ops:
  7.2 1.2 fusion.92
  9.3 1.3 fusion.94
  12.0 42.2 %all-gather.2.cloned.1.call-done = bf16[256,2,2048]{2,0,1:T(8,128)(2,1)} async-done(((bf16[16,2,2048]{2,0,1:T(8,128)(2,1)}), bf16[256,2,2048]{2,0,1:T(8,128)(2,1)}) %all-gather.2.cloned.1.call-update) | async-done | bytes 2097168 | tf_op jit(solution)/shard_map/all_gather | solution.py:104
  54.1 1.9 broadcast_select_fusion.1
  56.0 1.5 copy.19
  57.4 1.5 copy.20
  60.6 1.3 compare_select_fusion.6
  61.9 3.9 %compare_select_fusion.7 = (f32[16]{0:T(128)S(1)}, f32[16]{0:T(128)S(1)}, f32[16]{0:T(128)S(1)}, f32[16]{0:T(128)S(1)}, f32[16]{0:T(128)S(1)}, /*index=5*/f32[16]{0:T(128)S(1)}) fusion(s32[24]{0:T(128)S(1)} %convert_reduce_fusion, f32[]{:T(128)} %bitcast.21, f32[]{:T(128)} %bitcast.30, f32[]{:T(128)} %bitcast.29, f32[]{:T(128)} %bitcast.28, f32[]{:T(128)} %bitcast.26, ...), kind=kLoop, calls=%fused_computation.151 | loop fusion | flops 192 | bytes 856 | tf_op jit(solution)/shard_map/mul | solution.py:69
  65.8 4.1 %fusion.83 = (f32[2048,128]{1,0:T(8,128)S(1)}, f32[2048,128]{1,0:T(8,128)S(1)}) fusion(s32[128]{0:T(128)S(1)} %iota_add_fusion), kind=kLoop, calls=%fused_computation.130 | loop fusion | flops 3932160 | bytes 2097664 | tf_op jit(solution)/shard_map/cos | solution.py:40
  70.2 95.0 %all-reduce.3.cloned.1.call-done = (bf16[8,32,2,2048]{3,1,2,0:T(8,128)(2,1)}, bf16[8,32,2,2048]{3,1,2,0:T(8,128)(2,1)}) async-done(((bf16[8,32,2,2048]{3,1,2,0:T(8,128)(2,1)}, bf16[8,32,2,2048]{3,1,2,0:T(8,128)(2,1)}), (bf16[8,32,2,2048]{3,1,2,0:T(8,128)(2,1)}, bf16[8,32,2,2048]{3,1,2,0:T(8,128)(2,1)})) %all-reduce.3.cloned.1.call-update) | async-done | bytes 4194320 | tf_op jit(solution)/shard_map/psum | solution.py:10
  165.4 29.9 %while.21 = (s32[]{:T(128)}, f32[8,32,16,128]{3,2,1,0:T(8,128)S(1)}, bf16[8,32,2,2048]{3,1,2,0:T(8,128)(2,1)}, bf16[16,2,2048]{2,0,1:T(8,128)(2,1)S(1)}, bf16[4096,128]{1,0:T(8,128)(2,1)S(1)}, /*index=5*/s32[]{:T(128)}) while((s32[]{:T(128)}, f32[8,32,16,128]{3,2,1,0:T(8,128)S(1)}, bf16[8,32,2,2048]{3,1,2,0:T(8,128)(2,1)}, ...), condition=%wide.region_5.6_spmd, body=%wide.region_4.5_spmd.sunk | while | flops 553844736 | bytes 12189773 | solution.py:108
  165.4 1.0 dynamic-slice_bitcast_fusion.5
  166.4 1.4 add_convert_fusion.5
  167.9 1.2 fusion.110
  169.1 1.0 dynamic-slice_bitcast_fusion.5
  170.2 1.4 add_convert_fusion.5
  171.6 1.2 fusion.110
  172.9 1.0 dynamic-slice_bitcast_fusion.5
  173.9 1.4 add_convert_fusion.5
  175.3 1.2 fusion.110
  176.6 1.0 dynamic-slice_bitcast_fusion.5
  177.7 1.4 add_convert_fusion.5
  179.1 1.2 fusion.110
  180.4 1.0 dynamic-slice_bitcast_fusion.5
  181.4 1.4 add_convert_fusion.5
  182.8 1.2 fusion.110
  184.1 1.0 dynamic-slice_bitcast_fusion.5
  185.1 1.4 add_convert_fusion.5
  186.6 1.2 fusion.110
  187.8 1.0 dynamic-slice_bitcast_fusion.5
  188.9 1.4 add_convert_fusion.5
  190.3 1.2 fusion.110
  192.6 1.4 add_convert_fusion.5
  194.1 1.2 fusion.110
  195.3 1.3 copy-done.1
  196.8 29.9 %while.20 = (s32[]{:T(128)}, f32[8,32,16,128]{3,2,1,0:T(8,128)S(1)}, bf16[8,32,2,2048]{3,1,2,0:T(8,128)(2,1)}, bf16[16,2,2048]{2,0,1:T(8,128)(2,1)S(1)}, bf16[4096,128]{1,0:T(8,128)(2,1)S(1)}, /*index=5*/s32[]{:T(128)}) while((s32[]{:T(128)}, f32[8,32,16,128]{3,2,1,0:T(8,128)S(1)}, bf16[8,32,2,2048]{3,1,2,0:T(8,128)(2,1)}, ...), condition=%wide.region_2.3_spmd, body=%wide.region_1.2_spmd.sunk | while | flops 553844736 | bytes 12189773 | solution.py:108
  197.9 1.4 add_convert_fusion.4
  199.3 1.2 fusion.106
  201.6 1.4 add_convert_fusion.4
  203.0 1.2 fusion.106
  205.4 1.4 add_convert_fusion.4
  206.8 1.2 fusion.106
  209.1 1.4 add_convert_fusion.4
  210.5 1.2 fusion.106
  212.8 1.4 add_convert_fusion.4
  214.3 1.2 fusion.106
  216.6 1.4 add_convert_fusion.4
  218.0 1.2 fusion.106
  220.3 1.4 add_convert_fusion.4
  221.8 1.2 fusion.106
  224.1 1.4 add_convert_fusion.4
  225.5 1.2 fusion.106
  226.8 2.7 fusion.28
  229.7 4.1 %collective-permute-start = (f32[256,4,128]{2,1,0:T(4,128)S(1)}, f32[256,4,128]{2,1,0:T(4,128)S(1)}, u32[]{:S(2)}, u32[]{:S(2)}) collective-permute-start(f32[256,4,128]{2,1,0:T(4,128)S(1)} %get-tuple-element.92), channel_id=1, source_target_pairs={{0,1},{1,2},{2,3},{3,4},{4,5},{5,6},{6,7},{7,8},{8,9},{9,10},{10,1... | collective-permute-start | bytes 1572872 | tf_op jit(solution)/shard_map/ppermute | solution.py:18
  233.8 2.1 collective-permute-start.1
  236.1 3.6 %collective-permute-start.2 = (f32[256,4,128]{2,1,0:T(4,128)S(1)}, f32[256,4,128]{2,1,0:T(4,128)S(1)}, u32[]{:S(2)}, u32[]{:S(2)}) collective-permute-start(f32[256,4,128]{2,1,0:T(4,128)S(1)} %get-tuple-element.96), channel_id=1, source_target_pairs={{0,1},{1,2},{2,3},{3,4},{4,5},{5,6},{6,7},{7,8},{8,9},{9,10},{10,1... | collective-permute-start | bytes 1572872 | tf_op jit(solution)/shard_map/ppermute | solution.py:18
  239.7 1.9 collective-permute-start.3
  242.1 2.3 pad_maximum_fusion
  244.4 1.1 collective-permute-done
  245.5 8.8 %collective-permute-done.1 = f32[256,4,128]{2,1,0:T(4,128)S(1)} collective-permute-done((f32[256,4,128]{2,1,0:T(4,128)S(1)}, f32[256,4,128]{2,1,0:T(4,128)S(1)}, u32[]{:S(2)}, u32[]{:S(2)}) %collective-permute-start.1) | collective-permute-done | bytes 524320 | tf_op jit(solution)/shard_map/ppermute | solution.py:21
  254.3 3.9 %fusion.55 = f32[1,256,16,128]{3,2,1,0:T(8,128)S(1)} fusion(f32[256,16,128]{2,1,0:T(8,128)S(1)} %get-tuple-element.94, f32[256,4,128]{2,1,0:T(4,128)S(1)} %collective-permute-done.1, f32[256,4,128]{2,1,0:T(4,128)S(1)} %collective-permute-done, f32[16]{0:T(128)S(1)} %get-tuple-element.122, f32[16]{0:T(128)S(1)} %get-tuple-element.107, ...), kind=kLoop, calls=%fused_computation.91 | loop fusion | flops 13107200 | bytes 5243396 | tf_op jit(solution)/shard_map/stack | solution.py:115
  258.2 1.7 collective-permute-done.3
  259.9 3.9 %fusion.34 = f32[1,256,16,128]{3,2,1,0:T(8,128)S(1)} fusion(f32[256,16,128]{2,1,0:T(8,128)S(1)} %get-tuple-element.95, f32[256,4,128]{2,1,0:T(4,128)S(1)} %collective-permute-done.3, f32[256,4,128]{2,1,0:T(4,128)S(1)} %collective-permute-done.2, f32[16]{0:T(128)S(1)} %get-tuple-element.122, f32[16]{0:T(128)S(1)} %get-tuple-element.107, ...), kind=kLoop, calls=%fused_computation.70 | loop fusion | flops 13107200 | bytes 5243396 | tf_op jit(solution)/shard_map/stack | solution.py:115
  263.8 2.3 pad_maximum_fusion.1
  (72 shorter events, 13.6 us)
Async XLA Ops:
  7.2 47.0 %all-gather.2.cloned.1.call-start = ((), (), s32[]{:S(2)}) async-start(), calls=%async_computation | async-start | bytes 2228224 | tf_op jit(solution)/shard_map/all_gather | solution.py:104
  9.2 155.9 %all-reduce.3.cloned.1.call-start = ((), (), s32[]{:S(2)}) async-start(), calls=%async_computation.1 | async-start | bytes 8388608 | tf_op jit(solution)/shard_map/psum | solution.py:10
  58.9 0.7 copy-start.5
  58.9 0.9 copy-start.4
  70.0 95.4 %copy-start = (bf16[16,2,2048]{2,0,1:T(8,128)(2,1)S(1)}, bf16[16,2,2048]{2,0,1:T(8,128)(2,1)}, u32[]{:S(2)}) copy-start(bf16[16,2,2048]{2,0,1:T(8,128)(2,1)} %pad_maximum_fusion.6) | copy-start | bytes 393220
  195.3 1.3 copy-start.1
  229.5 12.2 %copy-start.2 = (f32[8,32,16,128]{3,2,1,0:T(8,128)S(1)}, f32[8,32,16,128]{3,2,1,0:T(8,128)}, u32[]{:S(2)}) copy-start(f32[8,32,16,128]{3,2,1,0:T(8,128)} %copy-done.1) | copy-start | bytes 6291460
  229.5 12.2 %copy-start.3 = (bf16[2,256,16,128]{3,2,1,0:T(8,128)(2,1)S(1)}, bf16[2,256,16,128]{3,2,1,0:T(8,128)(2,1)}, u32[]{:S(2)}) copy-start(bf16[2,256,16,128]{3,2,1,0:T(8,128)(2,1)} %param.10) | copy-start | bytes 6291460
  229.7 15.8 %collective-permute-start = (f32[256,4,128]{2,1,0:T(4,128)S(1)}, f32[256,4,128]{2,1,0:T(4,128)S(1)}, u32[]{:S(2)}, u32[]{:S(2)}) collective-permute-start(f32[256,4,128]{2,1,0:T(4,128)S(1)} %get-tuple-element.92), channel_id=1, source_target_pairs={{0,1},{1,2},{2,3},{3,4},{4,5},{5,6},{6,7},{7,8},{8,9},{9,10},{10,1... | collective-permute-start | bytes 1572872 | tf_op jit(solution)/shard_map/ppermute | solution.py:18
  233.8 20.5 %collective-permute-start.1 = (f32[256,4,128]{2,1,0:T(4,128)S(1)}, f32[256,4,128]{2,1,0:T(4,128)S(1)}, u32[]{:S(2)}, u32[]{:S(2)}) collective-permute-start(f32[256,4,128]{2,1,0:T(4,128)S(1)} %get-tuple-element.93), channel_id=1, source_target_pairs={{1,0},{2,1},{3,2},{4,3},{5,4},{6,5},{7,6},{8,7},{9,8},{10,9},{11,1... | collective-permute-start | bytes 1572872 | tf_op jit(solution)/shard_map/ppermute | solution.py:21
  236.1 22.2 %collective-permute-start.2 = (f32[256,4,128]{2,1,0:T(4,128)S(1)}, f32[256,4,128]{2,1,0:T(4,128)S(1)}, u32[]{:S(2)}, u32[]{:S(2)}) collective-permute-start(f32[256,4,128]{2,1,0:T(4,128)S(1)} %get-tuple-element.96), channel_id=1, source_target_pairs={{0,1},{1,2},{2,3},{3,4},{4,5},{5,6},{6,7},{7,8},{8,9},{9,10},{10,1... | collective-permute-start | bytes 1572872 | tf_op jit(solution)/shard_map/ppermute | solution.py:18
  239.7 20.2 %collective-permute-start.3 = (f32[256,4,128]{2,1,0:T(4,128)S(1)}, f32[256,4,128]{2,1,0:T(4,128)S(1)}, u32[]{:S(2)}, u32[]{:S(2)}) collective-permute-start(f32[256,4,128]{2,1,0:T(4,128)S(1)} %get-tuple-element.97), channel_id=1, source_target_pairs={{1,0},{2,1},{3,2},{4,3},{5,4},{6,5},{7,6},{8,7},{9,8},{10,9},{11,1... | collective-permute-start | bytes 1572872 | tf_op jit(solution)/shard_map/ppermute | solution.py:21
Sparse Core Ops, SparseCore 0:
  10.2 43.9 all-gather.1
  59.1 106.0 all-reduce.2
where the time goes:
time: 274 us; the launch traced here: 273 us
  waiting for transfers between devices  149 us (54%)
  other arithmetic  51.5 us (19%)
  local copies, waits for them, and re-layouts  24.5 us (9%)
  matrix products  20 us (7%)
  between operations  15.6 us (6%)
  starting transfers between devices  11.8 us (4%)
    psum x1, waiting for transfers between devices, from_root(): return lax.psum(kept, axis)  95 us
    all_gather x1, waiting for transfers between devices, shards(): whole = lax.all_gather(own, 'dev', axis=0, tiled=True)  42.2 us
    another operation x18, other arithmetic  22.8 us
    dot_general x16, matrix products, cross_block(): result = jnp.dot(flat, table, preferred_element_type=jnp.float32)  20 us
    squeeze x16, local copies, waits for them, and re-layouts, shards(): corr = lax.map(lambda block: cross_block(block, own, table), grouped)  15.5 us
    ppermute x2, waiting for transfers between devices, extended_2(): lax.ppermute(lax.slice_in_dim(block, 0, width, axis=dim), axis, backward)  10.5 us
    another operation x3, other arithmetic, shards(): filtered = jnp.stack(filtered_list, axis=0)  10.1 us
    ppermute x2, starting transfers between devices, extended_2(): lax.ppermute(lax.slice_in_dim(block, block.shape[dim] - width, None, axis...  7.73 us
  transfers between devices with their start and end apart: 6, of which 5 were waited for; matrix products, arithmetic and copies ran while one was open for 7% of the time, Pallas kernels for 0%

commit v1 on v0

--- a/solution.py
+++ b/solution.py
@@ -7,7 +7,7 @@
 
 def from_root(value, axis, source):
     kept = jnp.where(lax.axis_index(axis) == source, value, 0).astype(value.dtype)
-    return lax.psum(kept, axis)
+    return jnp.sum(lax.all_gather(kept, axis), axis=0)
 
 
 def extended_2(block, sides, width):

time: 274 us -> 254 us (0.927)
  waiting for transfers between devices: 149 us -> 121 us
  other arithmetic: 51.5 us -> 63.4 us
  local copies, waits for them, and re-layouts: 24.5 us -> 21.1 us
    psum x1 -> x0, waiting for transfers between devices: 95 us -> none  [from_root(): return lax.psum(kept, axis)]
    all_gather x0 -> x2, waiting for transfers between devices: none -> 66.8 us  [from_root(): return jnp.sum(lax.all_gather(kept, axis), axis=0)]
    reduce_sum x0 -> x2, other arithmetic: none -> 10.2 us  [from_root(): return jnp.sum(lax.all_gather(kept, axis), axis=0)]
    reshape x3 -> x1, local copies, waits for them, and re-layouts: 2.99 us -> 0.08 us  [the longest x2 2.91 us: shards(): grouped = sources.reshape(source_count // block_rows, block_rows, 2, freqs)]
  transfers between devices with their start and end apart: 6 -> 7, of which waited for: 5 -> 6; matrix products, arithmetic and copies ran while one was open for 7% -> 21% of each run, Pallas kernels for 0% -> 0%
where the time goes in v1:
time: 254 us; the launch traced here: 253 us
  waiting for transfers between devices  121 us (48%)
  other arithmetic  63.4 us (25%)
  local copies, waits for them, and re-layouts  21.1 us (8%)
  matrix products  20 us (8%)
  between operations  15.3 us (6%)
  starting transfers between devices  11.7 us (5%)
    all_gather x2, waiting for transfers between devices, from_root(): return jnp.sum(lax.all_gather(kept, axis), axis=0)  66.8 us
    all_gather x1, waiting for transfers between devices, shards(): whole = lax.all_gather(own, 'dev', axis=0, tiled=True)  42.2 us
    another operation x18, other arithmetic  22.8 us
    dot_general x16, matrix products, cross_block(): result = jnp.dot(flat, table, preferred_element_type=jnp.float32)  20 us
    squeeze x16, local copies, waits for them, and re-layouts, shards(): corr = lax.map(lambda block: cross_block(block, own, table), grouped)  15.7 us
    ppermute x2, waiting for transfers between devices, extended_2(): lax.ppermute(lax.slice_in_dim(block, 0, width, axis=dim), axis, backward)  10.5 us
    reduce_sum x2, other arithmetic, from_root(): return jnp.sum(lax.all_gather(kept, axis), axis=0)  10.2 us
    another operation x3, other arithmetic, shards(): filtered = jnp.stack(filtered_list, axis=0)  10 us
  transfers between devices with their start and end apart: 7, of which 6 were waited for; matrix products, arithmetic and copies ran while one was open for 21% of the time, Pallas kernels for 0%

profile of v1, /device:TPU:1, one launch (start us, length us, event | category | flops | bytes accessed | tf_op | source)
XLA Modules:
  0.0 253.1 jit_solution(4805661291233275801)
XLA Ops:
  7.2 1.2 fusion.92
  9.3 1.3 fusion.94
  12.0 42.2 %all-gather.6.cloned.1.call-done = bf16[256,2,2048]{2,0,1:T(8,128)(2,1)} async-done(((bf16[16,2,2048]{2,0,1:T(8,128)(2,1)}), bf16[256,2,2048]{2,0,1:T(8,128)(2,1)}) %all-gather.6.cloned.1.call-update) | async-done | bytes 2097168 | tf_op jit(solution)/shard_map/all_gather | solution.py:104
  54.1 3.9 %broadcast_select_fusion.1 = (bf16[256,2,2048]{2,0,1:T(8,128)(2,1)}, bf16[256,2,2048]{2,0,1:T(8,128)(2,1)}) fusion(bf16[256,2,2048]{2,0,1:T(8,128)(2,1)} %all-gather.6.cloned.1.call-done, pred[]{:T(512)S(6)} %eq.36, pred[]{:T(512)S(6)} %eq.37), kind=kLoop, calls=%fused_computation.119 | loop fusion | flops 2097152 | bytes 6291458 | tf_op jit(solution)/shard_map/jit(_where)/select_n | solution.py:9
  59.7 1.3 compare_select_fusion.6
  61.0 3.8 %compare_select_fusion.7 = (f32[16]{0:T(128)S(1)}, f32[16]{0:T(128)S(1)}, f32[16]{0:T(128)S(1)}, f32[16]{0:T(128)S(1)}, f32[16]{0:T(128)S(1)}, /*index=5*/f32[16]{0:T(128)S(1)}) fusion(s32[24]{0:T(128)S(1)} %convert_reduce_fusion, f32[]{:T(128)} %bitcast.23, f32[]{:T(128)} %bitcast.32, f32[]{:T(128)} %bitcast.31, f32[]{:T(128)} %bitcast.30, f32[]{:T(128)} %bitcast.28, ...), kind=kLoop, calls=%fused_computation.151 | loop fusion | flops 192 | bytes 856 | tf_op jit(solution)/shard_map/mul | solution.py:69
  64.8 4.1 %fusion.83 = (f32[2048,128]{1,0:T(8,128)S(1)}, f32[2048,128]{1,0:T(8,128)S(1)}) fusion(s32[128]{0:T(128)S(1)} %iota_add_fusion), kind=kLoop, calls=%fused_computation.130 | loop fusion | flops 3932160 | bytes 2097664 | tf_op jit(solution)/shard_map/cos | solution.py:40
  69.1 44.0 %all-gather.10.cloned.1.call-done = bf16[512,2,2048]{2,0,1:T(8,128)(2,1)} async-done(((bf16[256,2,2048]{2,0,1:T(8,128)(2,1)}), bf16[512,2,2048]{2,0,1:T(8,128)(2,1)}) %all-gather.10.cloned.1.call-update) | async-done | bytes 4194320 | tf_op jit(solution)/shard_map/all_gather | solution.py:10
  113.1 5.1 %reduce_sum.34 = bf16[256,2,2048]{2,0,1:T(8,128)(2,1)} reduce(bf16[2,256,2,2048]{3,1,0,2:T(8,128)(2,1)} %bitcast.115, bf16[]{:T(256)} %constant.100.clone.1), dimensions={0}, to_apply=%region_3.4 | reduce | flops 1048576 | bytes 6291458 | tf_op jit(solution)/shard_map/reduce_sum | solution.py:10
  119.1 30.0 %while.21 = (s32[]{:T(128)}, f32[8,32,16,128]{3,2,1,0:T(8,128)S(1)}, bf16[8,32,2,2048]{3,1,0,2:T(8,128)(2,1)}, bf16[16,2,2048]{2,0,1:T(8,128)(2,1)S(1)}, bf16[4096,128]{1,0:T(8,128)(2,1)S(1)}, /*index=5*/s32[]{:T(128)}) while((s32[]{:T(128)}, f32[8,32,16,128]{3,2,1,0:T(8,128)S(1)}, bf16[8,32,2,2048]{3,1,0,2:T(8,128)(2,1)}, ...), condition=%wide.region_5.6_spmd, body=%wide.region_4.5_spmd.sunk | while | flops 553844736 | bytes 12189773 | solution.py:108
  120.1 1.4 add_convert_fusion.5
  121.5 1.2 fusion.110
  122.8 1.0 dynamic-slice_bitcast_fusion.5
  123.9 1.4 add_convert_fusion.5
  125.3 1.2 fusion.110
  126.6 1.0 dynamic-slice_bitcast_fusion.5
  127.7 1.4 add_convert_fusion.5
  129.1 1.2 fusion.110
  130.4 1.0 dynamic-slice_bitcast_fusion.5
  131.4 1.4 add_convert_fusion.5
  132.8 1.2 fusion.110
  134.1 1.0 dynamic-slice_bitcast_fusion.5
  135.2 1.4 add_convert_fusion.5
  136.6 1.2 fusion.110
  138.9 1.4 add_convert_fusion.5
  140.3 1.2 fusion.110
  142.7 1.4 add_convert_fusion.5
  144.1 1.2 fusion.110
  145.4 1.0 dynamic-slice_bitcast_fusion.5
  146.4 1.4 add_convert_fusion.5
  147.8 1.2 fusion.110
  149.1 22.9 %all-gather.8.cloned.1.call-done = bf16[512,2,2048]{2,0,1:T(8,128)(2,1)} async-done(((bf16[256,2,2048]{2,0,1:T(8,128)(2,1)}), bf16[512,2,2048]{2,0,1:T(8,128)(2,1)}) %all-gather.8.cloned.1.call-update) | async-done | bytes 4194320 | tf_op jit(solution)/shard_map/all_gather | solution.py:10
  172.0 5.1 %reduce_sum.33 = bf16[256,2,2048]{2,0,1:T(8,128)(2,1)} reduce(bf16[2,256,2,2048]{3,1,0,2:T(8,128)(2,1)} %bitcast.116, bf16[]{:T(256)} %constant.100.clone.1), dimensions={0}, to_apply=%region_0.1 | reduce | flops 1048576 | bytes 6291458 | tf_op jit(solution)/shard_map/reduce_sum | solution.py:10
  177.2 30.0 %while.20 = (s32[]{:T(128)}, f32[8,32,16,128]{3,2,1,0:T(8,128)S(1)}, bf16[8,32,2,2048]{3,1,0,2:T(8,128)(2,1)}, bf16[16,2,2048]{2,0,1:T(8,128)(2,1)S(1)}, bf16[4096,128]{1,0:T(8,128)(2,1)S(1)}, /*index=5*/s32[]{:T(128)}) while((s32[]{:T(128)}, f32[8,32,16,128]{3,2,1,0:T(8,128)S(1)}, bf16[8,32,2,2048]{3,1,0,2:T(8,128)(2,1)}, ...), condition=%wide.region_2.3_spmd, body=%wide.region_1.2_spmd.sunk | while | flops 553844736 | bytes 12189773 | solution.py:108
  177.2 1.0 dynamic-slice_bitcast_fusion.4
  178.3 1.4 add_convert_fusion.4
  179.7 1.2 fusion.106
  182.0 1.4 add_convert_fusion.4
  183.5 1.2 fusion.106
  184.7 1.0 dynamic-slice_bitcast_fusion.4
  185.8 1.4 add_convert_fusion.4
  187.2 1.2 fusion.106
  189.5 1.4 add_convert_fusion.4
  191.0 1.2 fusion.106
  193.3 1.4 add_convert_fusion.4
  194.7 1.2 fusion.106
  197.0 1.4 add_convert_fusion.4
  198.5 1.2 fusion.106
  200.8 1.4 add_convert_fusion.4
  202.2 1.2 fusion.106
  204.5 1.4 add_convert_fusion.4
  205.9 1.2 fusion.106
  207.2 2.7 %fusion.28 = (f32[256,16,128]{2,1,0:T(8,128)S(1)}, f32[256,16,128]{2,1,0:T(8,128)S(1)}) fusion(f32[8,32,16,128]{3,2,1,0:T(8,128)S(1)} %get-tuple-element.56, bf16[2,256,16,128]{3,2,1,0:T(8,128)(2,1)} %param.10, f32[8,32,16,128]{3,2,1,0:T(8,128)} %copy-done.1), kind=kLoop, calls=%fused_computation.64 | loop fusion | flops 2097152 | bytes 10485760 | tf_op jit(solution)/shard_map/add | solution.py:110
  210.1 4.1 %collective-permute-start = (f32[256,4,128]{2,1,0:T(4,128)S(1)}, f32[256,4,128]{2,1,0:T(4,128)S(1)}, u32[]{:S(2)}, u32[]{:S(2)}) collective-permute-start(f32[256,4,128]{2,1,0:T(4,128)S(1)} %get-tuple-element.110), channel_id=1, source_target_pairs={{0,1},{1,2},{2,3},{3,4},{4,5},{5,6},{6,7},{7,8},{8,9},{9,10},{10,1... | collective-permute-start | bytes 1572872 | tf_op jit(solution)/shard_map/ppermute | solution.py:18
  214.2 1.9 collective-permute-start.1
  216.3 3.6 %collective-permute-start.2 = (f32[256,4,128]{2,1,0:T(4,128)S(1)}, f32[256,4,128]{2,1,0:T(4,128)S(1)}, u32[]{:S(2)}, u32[]{:S(2)}) collective-permute-start(f32[256,4,128]{2,1,0:T(4,128)S(1)} %get-tuple-element.114), channel_id=1, source_target_pairs={{0,1},{1,2},{2,3},{3,4},{4,5},{5,6},{6,7},{7,8},{8,9},{9,10},{10,1... | collective-permute-start | bytes 1572872 | tf_op jit(solution)/shard_map/ppermute | solution.py:18
  220.0 1.9 collective-permute-start.3
  222.4 2.3 pad_maximum_fusion
  224.7 1.2 collective-permute-done
  225.9 8.8 %collective-permute-done.1 = f32[256,4,128]{2,1,0:T(4,128)S(1)} collective-permute-done((f32[256,4,128]{2,1,0:T(4,128)S(1)}, f32[256,4,128]{2,1,0:T(4,128)S(1)}, u32[]{:S(2)}, u32[]{:S(2)}) %collective-permute-start.1) | collective-permute-done | bytes 524320 | tf_op jit(solution)/shard_map/ppermute | solution.py:21
  234.7 3.9 %fusion.55 = f32[1,256,16,128]{3,2,1,0:T(8,128)S(1)} fusion(f32[256,16,128]{2,1,0:T(8,128)S(1)} %get-tuple-element.112, f32[256,4,128]{2,1,0:T(4,128)S(1)} %collective-permute-done.1, f32[256,4,128]{2,1,0:T(4,128)S(1)} %collective-permute-done, f32[16]{0:T(128)S(1)} %get-tuple-element.140, f32[16]{0:T(128)S(1)} %get-tuple-element.125, ...), kind=kLoop, calls=%fused_computation.91 | loop fusion | flops 13107200 | bytes 5243396 | tf_op jit(solution)/shard_map/stack | solution.py:115
  238.6 1.7 collective-permute-done.3
  240.4 3.9 %fusion.34 = f32[1,256,16,128]{3,2,1,0:T(8,128)S(1)} fusion(f32[256,16,128]{2,1,0:T(8,128)S(1)} %get-tuple-element.113, f32[256,4,128]{2,1,0:T(4,128)S(1)} %collective-permute-done.3, f32[256,4,128]{2,1,0:T(4,128)S(1)} %collective-permute-done.2, f32[16]{0:T(128)S(1)} %get-tuple-element.140, f32[16]{0:T(128)S(1)} %get-tuple-element.125, ...), kind=kLoop, calls=%fused_computation.70 | loop fusion | flops 13107200 | bytes 5243396 | tf_op jit(solution)/shard_map/stack | solution.py:115
  244.2 2.3 pad_maximum_fusion.1
  (75 shorter events, 14.3 us)
Async XLA Ops:
  7.2 47.0 %all-gather.6.cloned.1.call-start = ((), (), s32[]{:S(2)}) async-start(), calls=%async_computation | async-start | bytes 2228224 | tf_op jit(solution)/shard_map/all_gather | solution.py:104
  9.2 103.8 %all-gather.10.cloned.1.call-start = ((), (), s32[]{:S(2)}) async-start(), calls=%async_computation.2 | async-start | bytes 6291456 | tf_op jit(solution)/shard_map/all_gather | solution.py:10
  58.0 0.7 copy-start.5
  58.0 0.9 copy-start.4
  58.0 113.9 %all-gather.8.cloned.1.call-start = ((), (), s32[]{:S(2)}) async-start(), calls=%async_computation.1 | async-start | bytes 6291456 | tf_op jit(solution)/shard_map/all_gather | solution.py:10
  118.2 0.9 copy-start
  149.1 28.0 %copy-start.1 = (f32[8,32,16,128]{3,2,1,0:T(8,128)}, f32[8,32,16,128]{3,2,1,0:T(8,128)S(1)}, u32[]{:S(2)}) copy-start(f32[8,32,16,128]{3,2,1,0:T(8,128)S(1)} %get-tuple-element.57) | copy-start | bytes 6291460
  209.9 12.0 %copy-start.2 = (f32[8,32,16,128]{3,2,1,0:T(8,128)S(1)}, f32[8,32,16,128]{3,2,1,0:T(8,128)}, u32[]{:S(2)}) copy-start(f32[8,32,16,128]{3,2,1,0:T(8,128)} %copy-done.1) | copy-start | bytes 6291460
  209.9 12.0 %copy-start.3 = (bf16[2,256,16,128]{3,2,1,0:T(8,128)(2,1)S(1)}, bf16[2,256,16,128]{3,2,1,0:T(8,128)(2,1)}, u32[]{:S(2)}) copy-start(bf16[2,256,16,128]{3,2,1,0:T(8,128)(2,1)} %param.10) | copy-start | bytes 6291460
  210.1 15.8 %collective-permute-start = (f32[256,4,128]{2,1,0:T(4,128)S(1)}, f32[256,4,128]{2,1,0:T(4,128)S(1)}, u32[]{:S(2)}, u32[]{:S(2)}) collective-permute-start(f32[256,4,128]{2,1,0:T(4,128)S(1)} %get-tuple-element.110), channel_id=1, source_target_pairs={{0,1},{1,2},{2,3},{3,4},{4,5},{5,6},{6,7},{7,8},{8,9},{9,10},{10,1... | collective-permute-start | bytes 1572872 | tf_op jit(solution)/shard_map/ppermute | solution.py:18
  214.2 20.5 %collective-permute-start.1 = (f32[256,4,128]{2,1,0:T(4,128)S(1)}, f32[256,4,128]{2,1,0:T(4,128)S(1)}, u32[]{:S(2)}, u32[]{:S(2)}) collective-permute-start(f32[256,4,128]{2,1,0:T(4,128)S(1)} %get-tuple-element.111), channel_id=1, source_target_pairs={{1,0},{2,1},{3,2},{4,3},{5,4},{6,5},{7,6},{8,7},{9,8},{10,9},{11,1... | collective-permute-start | bytes 1572872 | tf_op jit(solution)/shard_map/ppermute | solution.py:21
  216.3 22.3 %collective-permute-start.2 = (f32[256,4,128]{2,1,0:T(4,128)S(1)}, f32[256,4,128]{2,1,0:T(4,128)S(1)}, u32[]{:S(2)}, u32[]{:S(2)}) collective-permute-start(f32[256,4,128]{2,1,0:T(4,128)S(1)} %get-tuple-element.114), channel_id=1, source_target_pairs={{0,1},{1,2},{2,3},{3,4},{4,5},{5,6},{6,7},{7,8},{8,9},{9,10},{10,1... | collective-permute-start | bytes 1572872 | tf_op jit(solution)/shard_map/ppermute | solution.py:18
  220.0 20.4 %collective-permute-start.3 = (f32[256,4,128]{2,1,0:T(4,128)S(1)}, f32[256,4,128]{2,1,0:T(4,128)S(1)}, u32[]{:S(2)}, u32[]{:S(2)}) collective-permute-start(f32[256,4,128]{2,1,0:T(4,128)S(1)} %get-tuple-element.115), channel_id=1, source_target_pairs={{1,0},{2,1},{3,2},{4,3},{5,4},{6,5},{7,6},{8,7},{9,8},{10,9},{11,1... | collective-permute-start | bytes 1572872 | tf_op jit(solution)/shard_map/ppermute | solution.py:21
Sparse Core Ops, SparseCore 0:
  10.2 43.9 all-gather.5
  58.1 54.8 all-gather.9
  115.2 56.7 all-gather.7
